TPU v7x, 128 devices: a whole 4x4x4 slice. The times are simulated.
128 devices in a mesh: grp: 4 (over y), col: 32 (over x, z, core).
Axes of the slice: x: 4, y: 4, z: 4, core: 2. Of those that a mesh axis runs over, the one named last changes fastest.
Arguments:
- blocks: bfloat16 [24576, 32, 1024], P(('grp', 'col'))
- i_index: int32 [24576], P(('grp', 'col')), may hold values from 0 to 63
- j_index: int32 [24576], P(('grp', 'col')), may hold values from 0 to 63
- k_index: int32 [24576], P(('grp', 'col')), may hold values from 0 to 15
- block_count: int32 [128], P(('grp', 'col')), may hold values from 24 to 192, as said below
- b_factor: float32 [65536, 256], P(('grp', 'col'))
- c_factor: float32 [16384, 256], P(('grp', 'col'))
Outputs:
- a_update: float32 [8192, 256], P(('grp', 'col'))
- b_update: float32 [65536, 256], P(('grp', 'col'))
Inputs may be any that keep to these rules, and one draw needn't show every extreme that they name: block_count[d] is the number of live slots of device d = 32 * (grp index) + (col index): its slots d * 192 to d * 192 + block_count[d] - 1; every other slot is ignored. Some device has exactly 192 live slots.
All inputs are finite; a program needn't handle non-finite values.
Results may differ from a plain program's by a relative error of at most 0.005.
The roundings to bfloat16 on the way count: a program that leaves them out, or rounds other values in their place, can miss the bound.
Values may be sent and summed in bfloat16 or wider, within the bound.
No kernel may reach another device: no remote copies, remote signals or barrier semaphores. Data moves between devices by JAX's collectives and lax.ppermute only.
A program may use at most 128 MiB of HBM per device.

v0:
```python
import jax
import jax.numpy as jnp
from jax import lax
from jax.sharding import PartitionSpec as P

A_DEV = 2


def solve_rows(gram, right_side):
    factor_low = lax.linalg.cholesky(gram)
    halfway = lax.linalg.triangular_solve(
        factor_low, right_side, left_side=False, lower=True, transpose_a=True
    )
    return lax.linalg.triangular_solve(
        factor_low, halfway, left_side=False, lower=True, transpose_a=False
    )


def mode_term(
    blocks,
    left_rows,
    left_index,
    tail_rows,
    tail_index,
    target_index,
    live_mask,
    targets,
    first_mode,
):
    block_edge = blocks.shape[1]
    rank_width = left_rows.shape[1]
    group_size = 16
    groups = blocks.shape[0] // group_size
    left_table = left_rows.reshape(-1, block_edge, rank_width)
    tail_table = tail_rows.reshape(-1, block_edge, rank_width)
    target_ids = jnp.arange(targets, dtype=jnp.int32)

    def one_step(running, inputs):
        tensor_group, left_idx, tail_idx, target_idx, alive_row = inputs
        left_blk = left_table[left_idx].astype(jnp.float32)
        tail_blk = tail_table[tail_idx].astype(jnp.float32)
        product = (left_blk[:, :, None, :] * tail_blk[:, None, :, :]).astype(jnp.bfloat16)
        if first_mode:
            result = jnp.einsum(
                "bim,bmr->bir",
                tensor_group,
                product.reshape(group_size, block_edge * block_edge, rank_width),
                preferred_element_type=jnp.float32,
            )
        else:
            result = jnp.einsum(
                "bijk,bikr->bjr",
                tensor_group.reshape(group_size, block_edge, block_edge, block_edge),
                product,
                preferred_element_type=jnp.float32,
            )
        select = (target_idx[None, :] == target_ids[:, None]).astype(jnp.float32) * alive_row[
            None, :
        ]
        update = jnp.dot(
            select,
            result.reshape(group_size, block_edge * rank_width),
            precision=lax.Precision.HIGHEST,
        )
        return (running + update, None)

    inputs = (
        blocks.reshape(groups, group_size, block_edge, block_edge * block_edge),
        left_index.reshape(groups, group_size),
        tail_index.reshape(groups, group_size),
        target_index.reshape(groups, group_size),
        live_mask.reshape(groups, group_size),
    )
    start_value = jnp.zeros((targets, block_edge * rank_width), jnp.float32)
    running, _ = lax.scan(one_step, start_value, inputs)
    return running.reshape(targets * block_edge, rank_width)


def on_device(blocks, i_index, j_index, k_index, block_count, b_factor, c_factor):
    highest = lax.Precision.HIGHEST
    block_edge = blocks.shape[1]
    gram_second, gram_third = lax.psum(
        (
            jnp.dot(b_factor.T, b_factor, precision=highest),
            jnp.dot(c_factor.T, c_factor, precision=highest),
        ),
        ("grp", "col"),
    )
    b_range, c_range = (
        lax.all_gather(b_factor.astype(jnp.bfloat16), "grp", axis=0, tiled=True),
        lax.all_gather(c_factor.astype(jnp.bfloat16), "grp", axis=0, tiled=True),
    )
    live_mask = (jnp.arange(blocks.shape[0], dtype=jnp.int32) < block_count[0]).astype(jnp.float32)
    first_targets = A_DEV * lax.axis_size("col")
    second_targets = b_range.shape[0] // block_edge
    partial_value = mode_term(
        blocks, b_range, j_index, c_range, k_index, i_index, live_mask, first_targets, True
    )
    gram_one = gram_second * gram_third
    whole_sum = lax.psum(partial_value, "col")
    a_whole = solve_rows(gram_one, whole_sum)
    gram_first = lax.psum(jnp.dot(a_whole.T, a_whole, precision=highest), "grp")
    col_norm = jnp.sqrt(jnp.diagonal(gram_first) + 1e-06)
    a_range = (a_whole / col_norm[None, :]).astype(jnp.bfloat16)
    own_rows = A_DEV * block_edge
    a_update = lax.dynamic_slice_in_dim(a_whole, lax.axis_index("col") * own_rows, own_rows, 0)
    gram_two = gram_first / (col_norm[:, None] * col_norm[None, :]) * gram_third
    partial_two = mode_term(
        blocks, a_range, i_index, c_range, k_index, j_index, live_mask, second_targets, False
    )
    own_two = lax.psum_scatter(partial_two, "grp", scatter_dimension=0, tiled=True)
    b_update = solve_rows(gram_two, own_two)
    return (a_update, b_update)


def solution(mesh):
    return jax.shard_map(
        on_device,
        mesh=mesh,
        in_specs=(
            P(("grp", "col"), None, None),
            P(("grp", "col")),
            P(("grp", "col")),
            P(("grp", "col")),
            P(("grp", "col")),
            P(("grp", "col"), None),
            P(("grp", "col"), None),
        ),
        out_specs=(P(("grp", "col"), None), P(("grp", "col"), None)),
        check_vma=False,
    )
```

profile of v0, /device:TPU:0, one launch (start us, length us, event | category | flops | bytes accessed | tf_op | source)
XLA Modules:
  0.0 780.1 jit_solution(10742429783290168959)
XLA Ops:
  15.0 13.0 %all_gather.7 = bf16[512,256]{1,0:T(8,128)(2,1)S(1)} all-gather(bf16[128,256]{1,0:T(8,128)(2,1)S(1)} %convert_element_type.56), channel_id=1, replica_groups=mesh['grp'=4,'col'=32] {'grp'}, dimensions={0}, use_global_device_ids=true | all-gather | bytes 327680 | tf_op jit(solution)/shard_map/all_gather | solution.py:91
  28.0 135.6 %all-reduce.10.cloned.1.call-done = (f32[256,256]{0,1:T(8,128)}, f32[256,256]{0,1:T(8,128)}) async-done(((f32[256,256]{0,1:T(8,128)}, f32[256,256]{0,1:T(8,128)}), (f32[256,256]{0,1:T(8,128)}, f32[256,256]{0,1:T(8,128)})) %all-reduce.10.cloned.1.call-update) | async-done | bytes 524304 | tf_op jit(solution)/shard_map/psum | solution.py:82
  164.8 11.7 %custom-call.29 = f32[128,128]{1,0:T(8,128)S(1)} custom-call(f32[128,128]{1,0:T(8,128)S(1)} %slice.101), custom_call_target="Cholesky" | custom-call | tf_op jit(solution)/shard_map/cholesky/custom-call.2 | solution.py:10
  176.6 9.8 %custom-call.30 = f32[1,128,128]{1,2,0:T(8,128)S(1)} custom-call(f32[1,128,128]{2,1,0:T(8,128)S(1)} %get-tuple-element.262), custom_call_target="InvertDiagBlocksLowerTriangular" | custom-call | tf_op jit(solution)/shard_map/cholesky/custom-call.7 | solution.py:10
  187.1 11.7 %custom-call.31 = f32[128,128]{1,0:T(8,128)S(1)} custom-call(f32[128,128]{1,0:T(8,128)S(1)} %convolution_subtract_fusion.5), custom_call_target="Cholesky" | custom-call | tf_op jit(solution)/shard_map/cholesky/custom-call.3 | solution.py:10
  198.9 141.3 %while.26 = (s32[]{:T(128)}, f32[64,8192]{1,0:T(8,128)S(1)}, s32[12,16]{1,0:T(8,128)S(1)}, f32[12,16]{1,0:T(8,128)S(1)}, bf16[12,16,32,1024]{3,2,1,0:T(8,128)(2,...) while((s32[]{:T(128)}, f32[64,8192]{1,0:T(8,128)S(1)}, ...), condition=%wide.region_1.0_spmd.clone, body=%wide.region_0.0_spmd.clone.sunk | while | flops 378802272 | bytes 27796492 | solution.py:75
  348.3 19.7 %custom-call.20 = f32[2,128,128]{1,2,0:T(8,128)S(1)} custom-call(f32[2,128,128]{2,1,0:T(8,128)S(1)} %get-tuple-element.116), custom_call_target="InvertDiagBlocksLowerTriangular" | custom-call | tf_op jit(solution)/shard_map/triangular_solve | solution.py:11
  368.0 80.2 %all-reduce.6.cloned.1.call-done = f32[2048,256]{1,0:T(8,128)} async-done(((f32[2048,256]{1,0:T(8,128)}), f32[2048,256]{1,0:T(8,128)}) %all-reduce.6.cloned.1.call-update) | async-done | bytes 2097168 | tf_op jit(solution)/shard_map/psum | solution.py:100
  461.2 40.8 %all-reduce.8.cloned.1.call-done = f32[256,256]{0,1:T(8,128)} async-done(((f32[256,256]{0,1:T(8,128)}), f32[256,256]{0,1:T(8,128)}) %all-reduce.8.cloned.1.call-update) | async-done | bytes 262160 | tf_op jit(solution)/shard_map/psum | solution.py:102
  507.1 195.0 %while.27 = (s32[]{:T(128)}, f32[64,8192]{1,0:T(8,128)S(1)}, s32[12,16]{1,0:T(8,128)}, f32[12,16]{1,0:T(8,128)}, bf16[12,16,32,1024]{3,2,1,0:T(8,128)(2,1)}, /*i...) while((s32[]{:T(128)}, f32[64,8192]{1,0:T(8,128)S(1)}, ...), condition=%wide.region_11.13_spmd.clone, body=%wide.region_10.12_spmd.clone.sunk | while | flops 378802272 | bytes 15213583 | solution.py:75
  508.4 4.4 reshape.345
  524.7 4.4 reshape.345
  540.9 4.4 reshape.345
  557.2 4.4 reshape.345
  573.4 4.4 reshape.345
  589.7 4.4 reshape.345
  622.2 4.4 reshape.345
  654.7 4.4 reshape.345
  670.9 4.4 reshape.345
  687.2 4.4 reshape.345
  706.2 11.7 %custom-call.32 = f32[128,128]{1,0:T(8,128)S(1)} custom-call(f32[128,128]{1,0:T(8,128)S(1)} %slice.104), custom_call_target="Cholesky" | custom-call | tf_op jit(solution)/shard_map/cholesky/custom-call.2 | solution.py:10
  718.0 9.8 %custom-call.33 = f32[1,128,128]{1,2,0:T(8,128)S(1)} custom-call(f32[1,128,128]{2,1,0:T(8,128)S(1)} %get-tuple-element.258), custom_call_target="InvertDiagBlocksLowerTriangular" | custom-call | tf_op jit(solution)/shard_map/cholesky/custom-call.7 | solution.py:10
  728.5 11.7 %custom-call.34 = f32[128,128]{1,0:T(8,128)S(1)} custom-call(f32[128,128]{1,0:T(8,128)S(1)} %convolution_subtract_fusion.4), custom_call_target="Cholesky" | custom-call | tf_op jit(solution)/shard_map/cholesky/custom-call.3 | solution.py:10
  746.9 19.8 %custom-call.21 = f32[2,128,128]{1,2,0:T(8,128)S(1)} custom-call(f32[2,128,128]{2,1,0:T(8,128)S(1)} %get-tuple-element.124), custom_call_target="InvertDiagBlocksLowerTriangular" | custom-call | tf_op jit(solution)/shard_map/triangular_solve | solution.py:11
  (439 shorter events, 346.4 us)
Async XLA Ops:
  8.0 5.2 copy-start.5
  8.0 6.0 copy-start.8
  8.0 6.0 copy-start.12
  8.0 6.8 copy-start.13
  8.0 6.9 copy-start.14
  8.0 155.5 %all-reduce.10.cloned.1.call-start = ((), (), s32[]{:S(2)}) async-start(), calls=%async_computation.5 | async-start | bytes 1048576 | tf_op jit(solution)/shard_map/psum | solution.py:82
  13.2 185.7 %all-gather.2.cloned.1.call-start = ((), (), s32[]{:S(2)}) async-start(), calls=%async_computation.1 | async-start | bytes 1310720 | tf_op jit(solution)/shard_map/all_gather | solution.py:90
  14.0 434.3 %all-reduce.6.cloned.1.call-start = ((), (), s32[]{:S(2)}) async-start(), calls=%async_computation.2 | async-start | bytes 4194304 | tf_op jit(solution)/shard_map/psum | solution.py:100
  340.2 1.5 copy-start.10
  340.2 1.5 copy-start.11
  341.8 160.2 %all-reduce.8.cloned.1.call-start = ((), (), s32[]{:S(2)}) async-start(), calls=%async_computation.3 | async-start | bytes 524288 | tf_op jit(solution)/shard_map/psum | solution.py:102
  348.3 103.3 %copy-start.7 = (f32[256,256]{1,0:T(8,128)}, f32[256,256]{1,0:T(8,128)S(1)}, u32[]{:S(2)}) copy-start(f32[256,256]{1,0:T(8,128)S(1)} %get-tuple-element.553) | copy-start | bytes 786436
  348.3 103.3 %copy-start.15 = (s32[2,2]{1,0:T(2,128)}, s32[2,2]{1,0:T(2,128)S(1)}, u32[]{:S(2)}) copy-start(s32[2,2]{1,0:T(2,128)S(1)} %get-tuple-element.571) | copy-start | bytes 52
  448.3 2.4 copy-start.6
  453.6 51.0 %copy-start = (f32[2048,128]{1,0:T(8,128)}, f32[2048,128]{1,0:T(8,128)S(1)}, u32[]{:S(2)}) copy-start(f32[2048,128]{1,0:T(8,128)S(1)} %fusion.48) | copy-start | bytes 3145732
  456.5 4.7 copy-start.2
  460.7 306.1 %reduce-scatter.2.cloned.1.call-start = ((), (), s32[]{:S(2)}) async-start(), calls=%async_computation.4 | async-start | bytes 2621440 | tf_op jit(solution)/shard_map/reduce_scatter | solution.py:111
  703.6 1.2 copy-start.1
  703.6 1.5 copy-start.3
  703.6 2.2 copy-start.4
  703.6 2.2 copy-start.9
  706.0 36.9 %copy-start.16 = (s32[2,2]{1,0:T(2,128)S(1)}, s32[2,2]{1,0:T(2,128)}, u32[]{:S(2)}) copy-start(s32[2,2]{1,0:T(2,128)} %copy-done.15) | copy-start | bytes 52
Sparse Core Ops, SparseCore 0:
  13.8 149.6 all-reduce.9
Sparse Core Ops, SparseCore 1:
  15.9 26.6 all-gather.1
  341.9 106.3 all-reduce.5
  460.8 41.2 all-reduce.7
  703.7 30.0 reduce-scatter.1
where the time goes:
time: 792 us; the launch traced here: 780 us
  waiting for transfers between devices  257 us (32%)
  local copies, waits for them, and re-layouts  166 us (21%)
  other arithmetic  162 us (20%)
  matrix products  159 us (20%)
  between operations  19.7 us (2%)
  blocking collectives  13 us (2%)
    psum x1, waiting for transfers between devices, on_device(): lax.psum((jnp.dot(b_factor.T, b_factor, precision=highest), jnp.dot(c_fac...  136 us
    psum x1, waiting for transfers between devices, on_device(): whole_sum = lax.psum(partial_value, 'col')  80.2 us
    another operation x13, other arithmetic, solve_rows(): factor_low = lax.linalg.cholesky(gram)  68.6 us
    dot_general x24, matrix products, one_step(): jnp.dot(select, result.reshape(group_size, block_edge * rank_width), prec...  55 us
    reshape x12, local copies, waits for them, and re-layouts, one_step(): tensor_group.reshape(group_size, block_edge, block_edge, block_edge)  52.3 us
    dot_general x12, matrix products, one_step(): jnp.einsum('bijk,bikr->bjr', tensor_group.reshape(group_size, block_edge,...  48.5 us
    convert_element_type x12, other arithmetic, one_step(): (left_blk[:, :, None, :] * tail_blk[:, None, :, :]).astype(jnp.bfloat16)  46.2 us
    gather x24, local copies, waits for them, and re-layouts, one_step(): left_blk = left_table[left_idx].astype(jnp.float32)  42.9 us
  transfers between devices with their start and end apart: 5, of which 3 were waited for; matrix products, arithmetic and copies ran while one was open for 15% of the time, Pallas kernels for 0%

commit v1 on v0

--- a/solution.py
+++ b/solution.py
@@ -4,6 +4,10 @@
 from jax.sharding import PartitionSpec as P
 
 A_DEV = 2
+
+
+def raise_numbers_here(page, axis_name):
+    return jnp.sum(lax.all_gather(page, axis_name), axis=0)
 
 
 def solve_rows(gram, right_side):
@@ -97,7 +101,7 @@
         blocks, b_range, j_index, c_range, k_index, i_index, live_mask, first_targets, True
     )
     gram_one = gram_second * gram_third
-    whole_sum = lax.psum(partial_value, "col")
+    whole_sum = raise_numbers_here(partial_value, "col")
     a_whole = solve_rows(gram_one, whole_sum)
     gram_first = lax.psum(jnp.dot(a_whole.T, a_whole, precision=highest), "grp")
     col_norm = jnp.sqrt(jnp.diagonal(gram_first) + 1e-06)

time: 792 us -> 742 us (0.937)
  waiting for transfers between devices: 257 us -> 191 us
  other arithmetic: 162 us -> 184 us
    all_gather x0 -> x1, waiting for transfers between devices: none -> 140 us  [raise_numbers_here(): return jnp.sum(lax.all_gather(page, axis_name), axis=0)]
    psum x1, waiting for transfers between devices: 136 us -> 0.03 us  [on_device(): lax.psum((jnp.dot(b_factor.T, b_factor, precision=highest), jnp.dot(c_fac...]
    psum x1 -> x0, waiting for transfers between devices: 80.2 us -> none  [on_device(): whole_sum = lax.psum(partial_value, 'col')]
    reduce_sum x0 -> x1, other arithmetic: none -> 21.2 us  [raise_numbers_here(): return jnp.sum(lax.all_gather(page, axis_name), axis=0)]
    all_gather x1, waiting for transfers between devices: 0.03 us -> 9.78 us  [on_device(): lax.all_gather(b_factor.astype(jnp.bfloat16), 'grp', axis=0, tiled=True)]
  transfers between devices with their start and end apart: 5 -> 5, of which waited for: 3 -> 3; matrix products, arithmetic and copies ran while one was open for 15% -> 36% of each run, Pallas kernels for 0% -> 0%
where the time goes in v1:
time: 742 us; the launch traced here: 733 us
  waiting for transfers between devices  191 us (26%)
  other arithmetic  184 us (25%)
  local copies, waits for them, and re-layouts  166 us (22%)
  matrix products  155 us (21%)
  between operations  19.3 us (3%)
  blocking collectives  13.4 us (2%)
    all_gather x1, waiting for transfers between devices, raise_numbers_here(): return jnp.sum(lax.all_gather(page, axis_name), axis=0)  140 us
    another operation x13, other arithmetic, solve_rows(): factor_low = lax.linalg.cholesky(gram)  68.7 us
    dot_general x24, matrix products, one_step(): jnp.dot(select, result.reshape(group_size, block_edge * rank_width), prec...  55 us
    reshape x12, local copies, waits for them, and re-layouts, one_step(): tensor_group.reshape(group_size, block_edge, block_edge, block_edge)  52.3 us
    dot_general x12, matrix products, one_step(): jnp.einsum('bijk,bikr->bjr', tensor_group.reshape(group_size, block_edge,...  48.5 us
    convert_element_type x12, other arithmetic, one_step(): (left_blk[:, :, None, :] * tail_blk[:, None, :, :]).astype(jnp.bfloat16)  46.2 us
    gather x24, local copies, waits for them, and re-layouts, one_step(): left_blk = left_table[left_idx].astype(jnp.float32)  42.9 us
    psum x1, waiting for transfers between devices, on_device(): gram_first = lax.psum(jnp.dot(a_whole.T, a_whole, precision=highest), 'grp')  40.6 us
  transfers between devices with their start and end apart: 5, of which 3 were waited for; matrix products, arithmetic and copies ran while one was open for 36% of the time, Pallas kernels for 0%

profile of v1, /device:TPU:0, one launch (start us, length us, event | category | flops | bytes accessed | tf_op | source)
XLA Modules:
  0.0 732.6 jit_solution(10082113581654510926)
XLA Ops:
  14.8 13.4 %all_gather.10 = bf16[512,256]{1,0:T(8,128)(2,1)S(1)} all-gather(bf16[128,256]{1,0:T(8,128)(2,1)S(1)} %convert_element_type.56), channel_id=1, replica_groups=mesh['grp'=4,'col'=32] {'grp'}, dimensions={0}, use_global_device_ids=true | all-gather | bytes 327680 | tf_op jit(solution)/shard_map/all_gather | solution.py:95
  28.2 9.8 %all-gather.3.cloned.1.call-done = bf16[2048,256]{1,0:T(8,128)(2,1)} async-done(((bf16[512,256]{1,0:T(8,128)(2,1)}), bf16[2048,256]{1,0:T(8,128)(2,1)}) %all-gather.3.cloned.1.call-update) | async-done | bytes 1048592 | tf_op jit(solution)/shard_map/all_gather | solution.py:94
  38.0 141.1 %while.26 = (s32[]{:T(128)}, f32[64,8192]{1,0:T(8,128)S(1)}, s32[12,16]{1,0:T(8,128)S(1)}, f32[12,16]{1,0:T(8,128)S(1)}, bf16[12,16,32,1024]{3,2,1,0:T(8,128)(2,...) while((s32[]{:T(128)}, f32[64,8192]{1,0:T(8,128)S(1)}, ...), condition=%wide.region_1.0_spmd.clone, body=%wide.region_0.0_spmd.clone.sunk | while | flops 378802272 | bytes 27796492 | solution.py:79
  182.2 11.7 %custom-call.29 = f32[128,128]{1,0:T(8,128)S(1)} custom-call(f32[128,128]{1,0:T(8,128)S(1)} %slice.101), custom_call_target="Cholesky" | custom-call | tf_op jit(solution)/shard_map/cholesky/custom-call.2 | solution.py:14
  194.0 9.8 %custom-call.30 = f32[1,128,128]{1,2,0:T(8,128)S(1)} custom-call(f32[1,128,128]{2,1,0:T(8,128)S(1)} %get-tuple-element.264), custom_call_target="InvertDiagBlocksLowerTriangular" | custom-call | tf_op jit(solution)/shard_map/cholesky/custom-call.7 | solution.py:14
  204.5 11.7 %custom-call.31 = f32[128,128]{1,0:T(8,128)S(1)} custom-call(f32[128,128]{1,0:T(8,128)S(1)} %convolution_subtract_fusion.5), custom_call_target="Cholesky" | custom-call | tf_op jit(solution)/shard_map/cholesky/custom-call.3 | solution.py:14
  222.5 19.7 %custom-call.20 = f32[2,128,128]{1,2,0:T(8,128)S(1)} custom-call(f32[2,128,128]{2,1,0:T(8,128)S(1)} %get-tuple-element.116), custom_call_target="InvertDiagBlocksLowerTriangular" | custom-call | tf_op jit(solution)/shard_map/triangular_solve | solution.py:15
  242.2 140.4 %all-gather.5.cloned.1.call-done = f32[32,2048,256]{2,1,0:T(8,128)} async-done(((f32[1,2048,256]{2,1,0:T(8,128)}), f32[32,2048,256]{2,1,0:T(8,128)}) %all-gather.5.cloned.1.call-update) | async-done | bytes 67108880 | tf_op jit(solution)/shard_map/all_gather | solution.py:10
  382.7 21.2 %reduce_sum.9 = f32[2048,256]{1,0:T(8,128)S(1)} reduce(f32[32,2048,256]{2,1,0:T(8,128)} %all-gather.5.cloned.1.call-done, f32[]{:T(128)} %constant.108.clone.1), dimensions={0}, to_apply=%region_2.3 | reduce | flops 16252928 | bytes 69206016 | tf_op jit(solution)/shard_map/reduce_sum | solution.py:10
  414.1 40.6 %all-reduce.5.cloned.1.call-done = f32[256,256]{0,1:T(8,128)} async-done(((f32[256,256]{0,1:T(8,128)}), f32[256,256]{0,1:T(8,128)}) %all-reduce.5.cloned.1.call-update) | async-done | bytes 262160 | tf_op jit(solution)/shard_map/psum | solution.py:106
  459.9 195.1 %while.27 = (s32[]{:T(128)}, f32[64,8192]{1,0:T(8,128)S(1)}, s32[12,16]{1,0:T(8,128)}, f32[12,16]{1,0:T(8,128)}, bf16[12,16,32,1024]{3,2,1,0:T(8,128)(2,1)}, /*i...) while((s32[]{:T(128)}, f32[64,8192]{1,0:T(8,128)S(1)}, ...), condition=%wide.region_11.13_spmd.clone, body=%wide.region_10.12_spmd.clone.sunk | while | flops 378802272 | bytes 15213583 | solution.py:79
  477.6 4.4 reshape.341
  493.8 4.4 reshape.341
  510.1 4.4 reshape.341
  526.3 4.4 reshape.341
  542.6 4.4 reshape.341
  575.1 4.4 reshape.341
  607.6 4.4 reshape.341
  623.8 4.4 reshape.341
  640.0 4.4 reshape.341
  659.1 11.7 %custom-call.32 = f32[128,128]{1,0:T(8,128)S(1)} custom-call(f32[128,128]{1,0:T(8,128)S(1)} %slice.104), custom_call_target="Cholesky" | custom-call | tf_op jit(solution)/shard_map/cholesky/custom-call.2 | solution.py:14
  670.9 9.8 %custom-call.33 = f32[1,128,128]{1,2,0:T(8,128)S(1)} custom-call(f32[1,128,128]{2,1,0:T(8,128)S(1)} %get-tuple-element.260), custom_call_target="InvertDiagBlocksLowerTriangular" | custom-call | tf_op jit(solution)/shard_map/cholesky/custom-call.7 | solution.py:14
  681.4 11.7 %custom-call.34 = f32[128,128]{1,0:T(8,128)S(1)} custom-call(f32[128,128]{1,0:T(8,128)S(1)} %convolution_subtract_fusion.4), custom_call_target="Cholesky" | custom-call | tf_op jit(solution)/shard_map/cholesky/custom-call.3 | solution.py:14
  699.9 19.9 %custom-call.21 = f32[2,128,128]{1,2,0:T(8,128)S(1)} custom-call(f32[2,128,128]{2,1,0:T(8,128)S(1)} %get-tuple-element.124), custom_call_target="InvertDiagBlocksLowerTriangular" | custom-call | tf_op jit(solution)/shard_map/triangular_solve | solution.py:15
  (440 shorter events, 348.0 us)
Async XLA Ops:
  8.0 4.1 copy-start.5
  8.0 5.9 copy-start.8
  8.0 5.9 copy-start.12
  8.0 6.6 copy-start.13
  8.0 6.7 copy-start.14
  8.0 29.9 %all-gather.3.cloned.1.call-start = ((), (), s32[]{:S(2)}) async-start(), calls=%async_computation.1 | async-start | bytes 1310720 | tf_op jit(solution)/shard_map/all_gather | solution.py:94
  9.9 171.0 %all-reduce.7.cloned.1.call-start = ((), (), s32[]{:S(2)}) async-start(), calls=%async_computation.5 | async-start | bytes 1048576 | tf_op jit(solution)/shard_map/psum | solution.py:86
  13.8 368.8 %all-gather.5.cloned.1.call-start = ((), (), s32[]{:S(2)}) async-start(), calls=%async_computation.2 | async-start | bytes 69206016 | tf_op jit(solution)/shard_map/all_gather | solution.py:10
  179.1 1.5 copy-start.10
  179.2 1.5 copy-start.11
  180.7 274.1 %all-reduce.5.cloned.1.call-start = ((), (), s32[]{:S(2)}) async-start(), calls=%async_computation.3 | async-start | bytes 524288 | tf_op jit(solution)/shard_map/psum | solution.py:106
  222.5 160.1 %copy-start.6 = (f32[256,256]{1,0:T(8,128)}, f32[256,256]{1,0:T(8,128)S(1)}, u32[]{:S(2)}) copy-start(f32[256,256]{1,0:T(8,128)S(1)} %get-tuple-element.554) | copy-start | bytes 786436
  222.5 160.1 %copy-start.15 = (s32[2,2]{1,0:T(2,128)}, s32[2,2]{1,0:T(2,128)S(1)}, u32[]{:S(2)}) copy-start(s32[2,2]{1,0:T(2,128)S(1)} %get-tuple-element.572) | copy-start | bytes 52
  403.9 1.0 copy-start.7
  407.9 49.5 %copy-start = (f32[2048,128]{1,0:T(8,128)}, f32[2048,128]{1,0:T(8,128)S(1)}, u32[]{:S(2)}) copy-start(f32[2048,128]{1,0:T(8,128)S(1)} %fusion.48) | copy-start | bytes 3145732
  409.9 4.2 copy-start.2
  414.0 305.8 %reduce-scatter.2.cloned.1.call-start = ((), (), s32[]{:S(2)}) async-start(), calls=%async_computation.4 | async-start | bytes 2621440 | tf_op jit(solution)/shard_map/reduce_scatter | solution.py:115
  656.5 1.2 copy-start.1
  656.5 1.5 copy-start.3
  656.5 2.2 copy-start.4
  656.5 2.2 copy-start.9
  658.9 37.0 %copy-start.16 = (s32[2,2]{1,0:T(2,128)S(1)}, s32[2,2]{1,0:T(2,128)}, u32[]{:S(2)}) copy-start(s32[2,2]{1,0:T(2,128)} %copy-done.15) | copy-start | bytes 52
Sparse Core Ops, SparseCore 0:
  11.1 26.8 all-gather.2
  180.8 201.7 all-gather.4
  414.2 40.5 all-reduce.4
  656.6 30.1 reduce-scatter.1
Sparse Core Ops, SparseCore 1:
  15.4 148.4 all-reduce.6
